TPU v7x, 128 devices: a whole 4x4x4 slice. The times are simulated.
128 devices in a mesh: sx: 8 (over y, z_lo), sz: 16 (over x, z_hi, core).
Axes of the slice: x: 4, y: 4, z: 4 (z_hi: 2, z_lo: 2; z = z_hi * 2 + z_lo), core: 2. Of those that a mesh axis runs over, the one named last changes fastest.
Arguments:
- right_side: float32 [72, 256, 4096], P('sx', 'sz'), may hold values from -6 to 6
- coupling: bfloat16 [72, 5, 256, 256], P('sx'), may hold values from -0.15625 to 0.15625
- harmonic_offsets: int32 [5], replicated, may hold values from -6 to 6, as said below
- eigen_basis: bfloat16 [256, 256], replicated, may hold values from -0.375 to 0.375
- eigen_inverse: bfloat16 [256, 256], replicated, may hold values from -0.375 to 0.375
- eigen_size: float32 [256], replicated, may hold values from 0.5 to 50
Outputs:
- solution: float32 [72, 256, 4096], P('sx', 'sz')
Inputs may be any that keep to these rules, and one draw needn't show every extreme that they name: `harmonic_offsets`: the offsets are distinct; some offset equals 6 and some equals -6.
All inputs are finite; a program needn't handle non-finite values.
Results may differ from a plain program's by a relative error of at most 0.00065.
The roundings to bfloat16 on the way count: a program that leaves them out, or rounds other values in their place, can miss the bound.
Values may be sent and summed in bfloat16 or wider, within the bound.
A program may use at most 128 MiB of HBM per device.

v0:
```python
import jax
import jax.numpy as jnp
from jax import lax
from jax.sharding import PartitionSpec as P

KX = 72
KZ = 128
H = 5
OFF = 6
STEPS = 2
R = 32


def extended(value, sides, width):
    for axis, dim in sides:
        peers, length = (lax.axis_size(axis), value.shape[dim])
        up = [(i, (i + 1) % peers) for i in range(peers)]
        down = [(j, i) for i, j in up]
        last = lax.slice_in_dim(value, length - width, length, axis=dim)
        first = lax.slice_in_dim(value, 0, width, axis=dim)
        before = lax.ppermute(last, axis, up)
        after = lax.ppermute(first, axis, down)
        value = jnp.concatenate([before, value, after], axis=dim)
    return value


def wave_table(mode_count, span_count):
    first_mode = lax.axis_index("sx") * mode_count
    first_span = lax.axis_index("sz") * span_count
    modes = first_mode + jnp.arange(mode_count, dtype=jnp.int32)
    spans = first_span + jnp.arange(span_count, dtype=jnp.int32)
    signed_x = jnp.where(modes < KX // 2, modes, modes - KX).astype(jnp.float32) * (4.0 / KX)
    signed_z = jnp.where(spans < KZ // 2, spans, spans - KZ).astype(jnp.float32) * (4.0 / KZ)
    table = 1.0 + signed_x[:, None] ** 2 + signed_z[None, :] ** 2
    return jnp.repeat(table, R, axis=1)


def precondition(residual, eigen_basis, eigen_inverse, eigen_size, wave_square):
    rounded = residual.astype(jnp.bfloat16)
    spectral = jnp.einsum("ij,kjc->kic", eigen_inverse, rounded, preferred_element_type=jnp.float32)
    factor = -1.0 / (eigen_size[None, :, None] + wave_square[:, None, :])
    scaled = (spectral * factor).astype(jnp.bfloat16)
    result = jnp.einsum("ij,kjc->kic", eigen_basis, scaled, preferred_element_type=jnp.float32)
    return result.astype(jnp.bfloat16)


def apply_operator(search, coupling, harmonic_offsets, wave_square):
    mode_count = search.shape[0]
    padded = extended(search, (("sx", 0),), OFF)
    accum = -wave_square[:, None, :] * search.astype(jnp.float32)
    for harmonic in range(H):
        source = lax.dynamic_slice_in_dim(padded, OFF + harmonic_offsets[harmonic], mode_count, 0)
        accum = accum + jnp.einsum(
            "kij,kjc->kic", coupling[:, harmonic], source, preferred_element_type=jnp.float32
        )
    return accum


def relax(solution, residual, search_full, image):
    inner = jnp.sum(jnp.sum(image * residual, axis=(0, 1)).reshape(-1, R), axis=0)
    energy = jnp.sum(jnp.sum(image * image, axis=(0, 1)).reshape(-1, R), axis=0)
    aligned, total_energy = lax.psum((inner, energy), ("sx", "sz"))
    step_size = jnp.tile(aligned / (total_energy + 1e-06), image.shape[2] // R)
    return (solution + step_size * search_full, residual - step_size * image)


def shards(right_side, coupling, harmonic_offsets, eigen_basis, eigen_inverse, eigen_size):
    residual = lax.all_to_all(right_side, "sz", split_axis=2, concat_axis=1, tiled=True)
    wave_square = wave_table(residual.shape[0], residual.shape[2] // R)
    solution = jnp.zeros_like(residual)
    for sweep in range(STEPS):
        search = precondition(residual, eigen_basis, eigen_inverse, eigen_size, wave_square)
        image = apply_operator(search, coupling, harmonic_offsets, wave_square)
        solution, residual = relax(solution, residual, search.astype(jnp.float32), image)
    return lax.all_to_all(solution, "sz", split_axis=1, concat_axis=2, tiled=True)


def solution(mesh):
    in_specs = (P("sx", "sz", None), P("sx", None, None, None), P(), P(), P(), P())
    out_specs = P("sx", "sz", None)
    return jax.shard_map(shards, mesh=mesh, in_specs=in_specs, out_specs=out_specs, check_vma=False)
```

profile of v0, /device:TPU:1, one launch (start us, length us, event | category | flops | bytes accessed | tf_op | source)
XLA Modules:
  0.0 424.5 jit_solution(962264210277215487)
XLA Ops:
  0.0 0.0 copy-start
  0.0 17.6 %copy.68 = f32[9,16,4096]{1,0,2:T(8,128)} copy(f32[9,16,4096]{2,1,0:T(8,128)} %param.6) | data formatting | bytes 4718592 | tf_op args[0]
  17.6 19.3 %reshape.75 = f32[16,1,36864]{2,1,0:T(1,128)} reshape(f32[4096,9,16]{2,1,0:T(8,128)} %bitcast.113) | data formatting | bytes 4718592
  36.9 9.1 %all-to-all-start = ((f32[16,1,36864]{2,1,0:T(1,128)}), f32[16,1,36864]{2,1,0:T(1,128)S(1)}, u32[]{:S(2)}, u32[]{:S(2)}) async-start(f32[16,1,36864]{2,1,0:T(1,128)} %reshape.75), calls=%async_computation | async-start | bytes 4718592 | tf_op jit(solution)/shard_map/all_to_all | solution.py:68
  46.1 0.1 broadcast_add_fusion
  46.1 0.1 broadcast_in_dim.2
  46.2 0.1 broadcast_in_dim_reshape.2
  46.3 31.0 %all-to-all-done = f32[16,1,36864]{2,1,0:T(1,128)S(1)} async-done(((f32[16,1,36864]{2,1,0:T(1,128)}), f32[16,1,36864]{2,1,0:T(1,128)S(1)}, u32[]{:S(2)}, u32[]{:S(2)}) %all-to-all-start) | async-done | bytes 2359328 | tf_op jit(solution)/shard_map/all_to_all | solution.py:68
  77.3 1.4 copy-done.4
  78.7 0.6 broadcast.95
  79.3 8.0 %reduce = f32[16,36864]{1,0:T(8,128)S(1)} reduce(f32[16,1,36864]{2,1,0:T(1,128)} %copy-done.4, f32[]{:T(128)} %broadcast.95), dimensions={1}, to_apply=%all_to_all.26.reduce_sub_computation | reduce | bytes 4718596 | tf_op jit(solution)/shard_map/all_to_all | solution.py:68
  87.3 21.2 %reshape.76 = f32[4096,9,16]{2,1,0:T(8,128)} reshape(f32[16,36864]{1,0:T(8,128)S(1)} %reduce) | data formatting | bytes 4718592
  108.5 18.9 %copy.70 = f32[9,16,16,256]{3,2,1,0:T(8,128)S(1)} copy(f32[9,16,16,256]{2,0,3,1:T(8,128)} %bitcast.112) | data formatting | bytes 4718592 | tf_op jit(solution)/shard_map/all_to_all | solution.py:68
  127.4 0.0 copy-start.7
  127.4 1.5 copy.71
  128.9 0.0 copy-done
  128.9 0.0 copy-done.6
  128.9 3.3 fusion.13
  132.2 2.4 fusion.89
  134.6 0.7 collective-permute-start
  135.3 2.8 collective-permute-start.1
  138.1 0.7 fusion.90
  145.0 23.4 %collective-permute-done = bf16[6,256,256]{2,1,0:T(8,128)(2,1)} collective-permute-done((bf16[6,256,256]{2,1,0:T(8,128)(2,1)}, bf16[6,256,256]{2,1,0:T(8,128)(2,1)}, u32[]{:S(2)}, u32[]{:S(2)}) %collective-permute-start) | collective-permute-done | bytes 786464 | tf_op jit(solution)/shard_map/ppermute | solution.py:21
  168.4 2.3 collective-permute-done.1
  170.7 2.2 pad_maximum_fusion
  172.9 0.0 slice-start.1
  172.9 1.9 fusion.21
  174.8 1.8 fusion.25
  176.5 0.0 slice-done
  176.5 0.0 slice-done.1
  176.6 0.5 fusion.29
  177.0 0.0 copy-start.1
  177.0 0.5 fusion.17
  177.5 0.8 copy-done.1
  178.3 2.7 multiply_reduce_fusion.2
  181.0 0.1 reshape.69
  181.1 0.1 reshape.70
  181.2 67.8 %all-reduce.1 = (f32[32]{0:T(128)S(1)}, f32[32]{0:T(128)S(1)}) all-reduce(f32[32]{0:T(128)S(1)} %reduce_sum.73, f32[32]{0:T(128)S(1)} %reduce_sum.75), channel_id=1, replica_groups=mesh['sx'=8,'sz'=16] {'sx','sz'}, use_global_device_ids=true, to_apply=%region_2.3 | all-reduce | flops 64 | bytes 512 | tf_op jit(solution)/shard_map/psum | solution.py:62
  249.0 0.1 mul.87
  249.1 3.8 fusion.14
  252.9 1.6 fusion.88
  254.5 0.3 collective-permute-start.2
  254.8 3.3 collective-permute-start.3
  258.2 29.7 %collective-permute-done.2 = bf16[6,256,256]{2,1,0:T(8,128)(2,1)S(1)} collective-permute-done((bf16[6,256,256]{2,1,0:T(8,128)(2,1)S(1)}, bf16[6,256,256]{2,1,0:T(8,128)(2,1)S(1)}, u32[]{:S(2)}, u32[]{:S(2)}) %collective-permute-start.2) | collective-permute-done | bytes 786464 | tf_op jit(solution)/shard_map/ppermute | solution.py:21
  287.9 1.9 collective-permute-done.3
  289.8 1.6 pad_maximum_fusion.1
  291.4 1.8 fusion.23
  293.2 0.5 fusion.27
  293.7 0.5 fusion.31
  294.1 0.0 copy-start.2
  294.1 0.0 copy-start.3
  294.2 0.5 fusion.19
  294.6 0.8 copy-done.2
  295.4 0.8 copy-done.3
  296.2 1.5 multiply_reduce_fusion
  297.7 0.1 reshape.71
  297.8 0.1 reshape.72
  297.9 65.3 %all-reduce = (f32[32]{0:T(128)S(1)}, f32[32]{0:T(128)S(1)}) all-reduce(f32[32]{0:T(128)S(1)} %reduce_sum.77, f32[32]{0:T(128)S(1)} %reduce_sum.79), channel_id=1, replica_groups=mesh['sx'=8,'sz'=16] {'sx','sz'}, use_global_device_ids=true, to_apply=%region_8.9 | all-reduce | flops 64 | bytes 512 | tf_op jit(solution)/shard_map/psum | solution.py:62
  363.2 0.1 mul.95
  363.3 2.0 fusion.5
  365.3 1.5 copy.80
  366.8 54.6 %all_to_all.36 = f32[9,256,256]{2,0,1:T(8,128)S(1)} all-to-all(f32[9,256,256]{2,0,1:T(8,128)S(1)} %copy.80), channel_id=1, replica_groups=mesh['sx'=8,'sz'=16] {'sz'}, dimensions={1} | all-to-all | bytes 4718592 | tf_op jit(solution)/shard_map/all_to_all | solution.py:75
  421.5 1.4 copy.81
  422.8 1.6 all_to_all.33
  (23 shorter events, 0.1 us)
Async XLA Ops:
  0.0 128.9 %copy-start = (bf16[256,256]{1,0:T(8,128)(2,1)S(1)}, bf16[256,256]{1,0:T(8,128)(2,1)}, u32[]{:S(2)}) copy-start(bf16[256,256]{1,0:T(8,128)(2,1)} %param.9) | copy-start | bytes 393220
  36.9 40.4 %all-to-all-start = ((f32[16,1,36864]{2,1,0:T(1,128)}), f32[16,1,36864]{2,1,0:T(1,128)S(1)}, u32[]{:S(2)}, u32[]{:S(2)}) async-start(f32[16,1,36864]{2,1,0:T(1,128)} %reshape.75), calls=%async_computation | async-start | bytes 4718592 | tf_op jit(solution)/shard_map/all_to_all | solution.py:68
  77.3 1.4 copy-start.4
  127.4 1.5 copy-start.6
  127.4 1.5 copy-start.7
  132.2 5.9 %copy-start.5 = (s32[5]{0:T(128)S(1)}, s32[5]{0:T(128)}, u32[]{:S(2)}) copy-start(s32[5]{0:T(128)} %param.8) | copy-start | bytes 64
  134.6 33.8 %collective-permute-start = (bf16[6,256,256]{2,1,0:T(8,128)(2,1)}, bf16[6,256,256]{2,1,0:T(8,128)(2,1)}, u32[]{:S(2)}, u32[]{:S(2)}) collective-permute-start(bf16[6,256,256]{2,1,0:T(8,128)(2,1)} %get-tuple-element.15), channel_id=1, source_target_pairs={{0,16},{16,32},{32,48},{48,64},{64,80},{80,96},{96,112},{112,0},{1... | collective-permute-start | bytes 2359304 | tf_op jit(solution)/shard_map/ppermute | solution.py:21
  135.3 35.4 %collective-permute-start.1 = (bf16[6,256,256]{2,1,0:T(8,128)(2,1)S(1)}, bf16[6,256,256]{2,1,0:T(8,128)(2,1)}, u32[]{:S(2)}, u32[]{:S(2)}) collective-permute-start(bf16[6,256,256]{2,1,0:T(8,128)(2,1)S(1)} %get-tuple-element.16), channel_id=1, source_target_pairs={{16,0},{32,16},{48,32},{64,48},{80,64},{96,80},{112,96},{0,112},{1... | collective-permute-start | bytes 2359304 | tf_op jit(solution)/shard_map/ppermute | solution.py:22
  170.7 5.9 %slice-start = ((s8[5898240]{0:T(1024)(128)(4,1)}), s8[4194304]{0:T(1024)(128)(4,1)S(1)}, s32[]{:S(2)}) async-start(s8[5898240]{0:T(1024)(128)(4,1)} %bitcast.116), calls=%async_computation.2 | async-start | bytes 8388608
  172.9 3.7 slice-start.1
  177.0 1.3 copy-start.1
  252.9 40.3 %slice-start.2 = ((s8[5898240]{0:T(1024)(128)(4,1)}), s8[4194304]{0:T(1024)(128)(4,1)S(1)}, s32[]{:S(2)}) async-start(s8[5898240]{0:T(1024)(128)(4,1)} %bitcast.118), calls=%async_computation.4 | async-start | bytes 8388608
  254.5 33.4 %collective-permute-start.2 = (bf16[6,256,256]{2,1,0:T(8,128)(2,1)S(1)}, bf16[6,256,256]{2,1,0:T(8,128)(2,1)S(1)}, u32[]{:S(2)}, u32[]{:S(2)}) collective-permute-start(bf16[6,256,256]{2,1,0:T(8,128)(2,1)S(1)} %get-tuple-element.13), channel_id=1, source_target_pairs={{0,16},{16,32},{32,48},{48,64},{64,80},{80,96},{96,112},{112,0},{1... | collective-permute-start | bytes 2359304 | tf_op jit(solution)/shard_map/ppermute | solution.py:21
  254.8 38.3 %slice-start.3 = ((s8[5898240]{0:T(1024)(128)(4,1)}), s8[1703936]{0:T(1024)(128)(4,1)S(1)}, s32[]{:S(2)}) async-start(s8[5898240]{0:T(1024)(128)(4,1)} %bitcast.118), calls=%async_computation.5 | async-start | bytes 3407872
  254.8 35.0 %collective-permute-start.3 = (bf16[6,256,256]{2,1,0:T(8,128)(2,1)S(1)}, bf16[6,256,256]{2,1,0:T(8,128)(2,1)S(1)}, u32[]{:S(2)}, u32[]{:S(2)}) collective-permute-start(bf16[6,256,256]{2,1,0:T(8,128)(2,1)S(1)} %get-tuple-element.14), channel_id=1, source_target_pairs={{16,0},{32,16},{48,32},{64,48},{80,64},{96,80},{112,96},{0,112},{1... | collective-permute-start | bytes 2359304 | tf_op jit(solution)/shard_map/ppermute | solution.py:22
  294.1 1.3 copy-start.2
  294.1 2.0 copy-start.3
where the time goes:
time: 426 us; the launch traced here: 424 us
  blocking collectives  188 us (44%)
  local copies, waits for them, and re-layouts  92.6 us (22%)
  waiting for transfers between devices  88.3 us (21%)
  matrix products  19.1 us (4%)
  starting transfers between devices  16.3 us (4%)
  other arithmetic  13.9 us (3%)
  between operations  6.39 us (2%)
    psum x2, blocking collectives, relax(): aligned, total_energy = lax.psum((inner, energy), ('sx', 'sz'))  133 us
    unnamed x27, local copies, waits for them, and re-layouts  61.9 us
    all_to_all x1, blocking collectives, shards(): lax.all_to_all(solution, 'sz', split_axis=1, concat_axis=2, tiled=True)  54.6 us
    ppermute x2, waiting for transfers between devices, extended(): before = lax.ppermute(last, axis, up)  53.1 us
    all_to_all x1, waiting for transfers between devices, shards(): lax.all_to_all(right_side, 'sz', split_axis=2, concat_axis=1, tiled=True)  31 us
    all_to_all x3, local copies, waits for them, and re-layouts, shards(): lax.all_to_all(right_side, 'sz', split_axis=2, concat_axis=1, tiled=True)  21 us
    dot_general x10, matrix products, apply_operator(): jnp.einsum('kij,kjc->kic', coupling[:, harmonic], source, preferred_eleme...  12 us
    all_to_all x1, starting transfers between devices, shards(): lax.all_to_all(right_side, 'sz', split_axis=2, concat_axis=1, tiled=True)  9.13 us
  transfers between devices with their start and end apart: 5, of which 5 were waited for; matrix products, arithmetic and copies ran while one was open for 0% of the time, Pallas kernels for 0%

commit v1 on v0

--- a/solution.py
+++ b/solution.py
@@ -59,7 +59,7 @@
 def relax(solution, residual, search_full, image):
     inner = jnp.sum(jnp.sum(image * residual, axis=(0, 1)).reshape(-1, R), axis=0)
     energy = jnp.sum(jnp.sum(image * image, axis=(0, 1)).reshape(-1, R), axis=0)
-    aligned, total_energy = lax.psum((inner, energy), ("sx", "sz"))
+    aligned, total_energy = lax.psum(lax.psum((inner, energy), "sz"), "sx")
     step_size = jnp.tile(aligned / (total_energy + 1e-06), image.shape[2] // R)
     return (solution + step_size * search_full, residual - step_size * image)
 

time: 426 us -> 391 us (0.918)
  blocking collectives: 188 us -> 154 us
    psum x2 -> x4, blocking collectives: 133 us -> 97.1 us  [relax(): aligned, total_energy = lax.psum(lax.psum((inner, energy), 'sz'), 'sx')]
where the time goes in v1:
time: 391 us; the launch traced here: 390 us
  blocking collectives  154 us (39%)
  local copies, waits for them, and re-layouts  92.7 us (24%)
  waiting for transfers between devices  87.4 us (22%)
  matrix products  19.1 us (5%)
  starting transfers between devices  16.3 us (4%)
  other arithmetic  13.9 us (4%)
  between operations  6.4 us (2%)
    psum x4, blocking collectives, relax(): aligned, total_energy = lax.psum(lax.psum((inner, energy), 'sz'), 'sx')  97.1 us
    unnamed x27, local copies, waits for them, and re-layouts  61.9 us
    all_to_all x1, blocking collectives, shards(): lax.all_to_all(solution, 'sz', split_axis=1, concat_axis=2, tiled=True)  56.9 us
    ppermute x2, waiting for transfers between devices, extended(): before = lax.ppermute(last, axis, up)  52.5 us
    all_to_all x1, waiting for transfers between devices, shards(): lax.all_to_all(right_side, 'sz', split_axis=2, concat_axis=1, tiled=True)  31 us
    all_to_all x3, local copies, waits for them, and re-layouts, shards(): lax.all_to_all(right_side, 'sz', split_axis=2, concat_axis=1, tiled=True)  21 us
    dot_general x10, matrix products, apply_operator(): jnp.einsum('kij,kjc->kic', coupling[:, harmonic], source, preferred_eleme...  12 us
    all_to_all x1, starting transfers between devices, shards(): lax.all_to_all(right_side, 'sz', split_axis=2, concat_axis=1, tiled=True)  9.13 us
  transfers between devices with their start and end apart: 5, of which 5 were waited for; matrix products, arithmetic and copies ran while one was open for 0% of the time, Pallas kernels for 0%

profile of v1, /device:TPU:1, one launch (start us, length us, event | category | flops | bytes accessed | tf_op | source)
XLA Modules:
  0.0 389.9 jit_solution(6144199565308395660)
XLA Ops:
  0.0 0.0 copy-start
  0.0 17.6 %copy.68 = f32[9,16,4096]{1,0,2:T(8,128)} copy(f32[9,16,4096]{2,1,0:T(8,128)} %param.6) | data formatting | bytes 4718592 | tf_op args[0]
  17.6 19.3 %reshape.75 = f32[16,1,36864]{2,1,0:T(1,128)} reshape(f32[4096,9,16]{2,1,0:T(8,128)} %bitcast.113) | data formatting | bytes 4718592
  36.9 9.1 %all-to-all-start = ((f32[16,1,36864]{2,1,0:T(1,128)}), f32[16,1,36864]{2,1,0:T(1,128)S(1)}, u32[]{:S(2)}, u32[]{:S(2)}) async-start(f32[16,1,36864]{2,1,0:T(1,128)} %reshape.75), calls=%async_computation | async-start | bytes 4718592 | tf_op jit(solution)/shard_map/all_to_all | solution.py:68
  46.1 0.1 broadcast_add_fusion
  46.1 0.1 broadcast_in_dim.2
  46.2 0.1 broadcast_in_dim_reshape.2
  46.3 31.0 %all-to-all-done = f32[16,1,36864]{2,1,0:T(1,128)S(1)} async-done(((f32[16,1,36864]{2,1,0:T(1,128)}), f32[16,1,36864]{2,1,0:T(1,128)S(1)}, u32[]{:S(2)}, u32[]{:S(2)}) %all-to-all-start) | async-done | bytes 2359328 | tf_op jit(solution)/shard_map/all_to_all | solution.py:68
  77.3 1.4 copy-done.4
  78.7 0.6 broadcast.95
  79.3 8.0 %reduce = f32[16,36864]{1,0:T(8,128)S(1)} reduce(f32[16,1,36864]{2,1,0:T(1,128)} %copy-done.4, f32[]{:T(128)} %broadcast.95), dimensions={1}, to_apply=%all_to_all.26.reduce_sub_computation | reduce | bytes 4718596 | tf_op jit(solution)/shard_map/all_to_all | solution.py:68
  87.3 21.2 %reshape.76 = f32[4096,9,16]{2,1,0:T(8,128)} reshape(f32[16,36864]{1,0:T(8,128)S(1)} %reduce) | data formatting | bytes 4718592
  108.5 18.9 %copy.70 = f32[9,16,16,256]{3,2,1,0:T(8,128)S(1)} copy(f32[9,16,16,256]{2,0,3,1:T(8,128)} %bitcast.112) | data formatting | bytes 4718592 | tf_op jit(solution)/shard_map/all_to_all | solution.py:68
  127.4 0.0 copy-start.7
  127.4 1.5 copy.71
  128.9 3.3 fusion.13
  132.2 2.4 fusion.89
  134.6 0.7 collective-permute-start
  135.3 2.8 collective-permute-start.1
  138.1 0.7 fusion.90
  145.0 23.4 %collective-permute-done = bf16[6,256,256]{2,1,0:T(8,128)(2,1)} collective-permute-done((bf16[6,256,256]{2,1,0:T(8,128)(2,1)}, bf16[6,256,256]{2,1,0:T(8,128)(2,1)}, u32[]{:S(2)}, u32[]{:S(2)}) %collective-permute-start) | collective-permute-done | bytes 786464 | tf_op jit(solution)/shard_map/ppermute | solution.py:21
  168.4 2.3 collective-permute-done.1
  170.7 2.2 pad_maximum_fusion
  172.9 0.0 slice-start.1
  172.9 1.9 fusion.21
  174.8 1.8 fusion.25
  176.5 0.0 slice-done
  176.5 0.0 slice-done.1
  176.6 0.5 fusion.29
  177.0 0.0 copy-start.1
  177.0 0.5 fusion.17
  177.5 0.8 copy-done.1
  178.3 2.7 multiply_reduce_fusion.2
  181.0 0.1 reshape.69
  181.1 0.1 reshape.70
  181.2 34.3 %all-reduce.1 = (f32[32]{0:T(128)S(1)}, f32[32]{0:T(128)S(1)}) all-reduce(f32[32]{0:T(128)S(1)} %reduce_sum.73, f32[32]{0:T(128)S(1)} %reduce_sum.75), channel_id=1, replica_groups=mesh['sx'=8,'sz'=16] {'sz'}, use_global_device_ids=true, to_apply=%region_2.3 | all-reduce | flops 64 | bytes 512 | tf_op jit(solution)/shard_map/psum | solution.py:62
  215.5 14.8 %all-reduce.3 = (f32[32]{0:T(128)S(1)}, f32[32]{0:T(128)S(1)}) all-reduce(f32[32]{0:T(128)S(1)} %get-tuple-element.11, f32[32]{0:T(128)S(1)} %get-tuple-element.12), channel_id=1, replica_groups=mesh['sx'=8,'sz'=16] {'sx'}, use_global_device_ids=true, to_apply=%region_3.4 | all-reduce | flops 64 | bytes 512 | tf_op jit(solution)/shard_map/psum | solution.py:62
  230.4 0.1 mul.87
  230.5 3.8 fusion.14
  234.3 1.6 fusion.88
  235.9 0.1 collective-permute-start.2
  236.0 0.0 slice-start.3
  236.0 3.6 collective-permute-start.3
  239.5 29.1 %collective-permute-done.2 = bf16[6,256,256]{2,1,0:T(8,128)(2,1)S(1)} collective-permute-done((bf16[6,256,256]{2,1,0:T(8,128)(2,1)S(1)}, bf16[6,256,256]{2,1,0:T(8,128)(2,1)S(1)}, u32[]{:S(2)}, u32[]{:S(2)}) %collective-permute-start.2) | collective-permute-done | bytes 786464 | tf_op jit(solution)/shard_map/ppermute | solution.py:21
  268.6 1.6 collective-permute-done.3
  270.3 1.6 pad_maximum_fusion.1
  271.9 1.8 fusion.23
  273.7 0.5 fusion.27
  274.1 0.5 fusion.31
  274.6 0.0 copy-start.3
  274.7 0.5 fusion.19
  275.1 0.8 copy-done.2
  275.9 0.8 copy-done.3
  276.7 1.5 multiply_reduce_fusion
  278.2 0.1 reshape.71
  278.3 0.1 reshape.72
  278.4 35.1 %all-reduce = (f32[32]{0:T(128)S(1)}, f32[32]{0:T(128)S(1)}) all-reduce(f32[32]{0:T(128)S(1)} %reduce_sum.77, f32[32]{0:T(128)S(1)} %reduce_sum.79), channel_id=1, replica_groups=mesh['sx'=8,'sz'=16] {'sz'}, use_global_device_ids=true, to_apply=%region_10.11 | all-reduce | flops 64 | bytes 512 | tf_op jit(solution)/shard_map/psum | solution.py:62
  313.5 12.9 %all-reduce.2 = (f32[32]{0:T(128)S(1)}, f32[32]{0:T(128)S(1)}) all-reduce(f32[32]{0:T(128)S(1)} %get-tuple-element.9, f32[32]{0:T(128)S(1)} %get-tuple-element.10), channel_id=1, replica_groups=mesh['sx'=8,'sz'=16] {'sx'}, use_global_device_ids=true, to_apply=%region_11.12 | all-reduce | flops 64 | bytes 512 | tf_op jit(solution)/shard_map/psum | solution.py:62
  326.3 0.1 mul.95
  326.4 2.0 fusion.5
  328.4 1.5 copy.80
  329.9 56.9 %all_to_all.36 = f32[9,256,256]{2,0,1:T(8,128)S(1)} all-to-all(f32[9,256,256]{2,0,1:T(8,128)S(1)} %copy.80), channel_id=1, replica_groups=mesh['sx'=8,'sz'=16] {'sz'}, dimensions={1} | all-to-all | bytes 4718592 | tf_op jit(solution)/shard_map/all_to_all | solution.py:75
  386.9 1.4 copy.81
  388.2 1.6 all_to_all.33
  (25 shorter events, 0.2 us)
Async XLA Ops:
  0.0 128.9 %copy-start = (bf16[256,256]{1,0:T(8,128)(2,1)S(1)}, bf16[256,256]{1,0:T(8,128)(2,1)}, u32[]{:S(2)}) copy-start(bf16[256,256]{1,0:T(8,128)(2,1)} %param.9) | copy-start | bytes 393220
  36.9 40.4 %all-to-all-start = ((f32[16,1,36864]{2,1,0:T(1,128)}), f32[16,1,36864]{2,1,0:T(1,128)S(1)}, u32[]{:S(2)}, u32[]{:S(2)}) async-start(f32[16,1,36864]{2,1,0:T(1,128)} %reshape.75), calls=%async_computation | async-start | bytes 4718592 | tf_op jit(solution)/shard_map/all_to_all | solution.py:68
  77.3 1.4 copy-start.4
  127.4 1.5 copy-start.6
  127.4 1.5 copy-start.7
  132.2 5.9 %copy-start.5 = (s32[5]{0:T(128)S(1)}, s32[5]{0:T(128)}, u32[]{:S(2)}) copy-start(s32[5]{0:T(128)} %param.8) | copy-start | bytes 64
  134.6 33.8 %collective-permute-start = (bf16[6,256,256]{2,1,0:T(8,128)(2,1)}, bf16[6,256,256]{2,1,0:T(8,128)(2,1)}, u32[]{:S(2)}, u32[]{:S(2)}) collective-permute-start(bf16[6,256,256]{2,1,0:T(8,128)(2,1)} %get-tuple-element.19), channel_id=1, source_target_pairs={{0,16},{16,32},{32,48},{48,64},{64,80},{80,96},{96,112},{112,0},{1... | collective-permute-start | bytes 2359304 | tf_op jit(solution)/shard_map/ppermute | solution.py:21
  135.3 35.4 %collective-permute-start.1 = (bf16[6,256,256]{2,1,0:T(8,128)(2,1)S(1)}, bf16[6,256,256]{2,1,0:T(8,128)(2,1)}, u32[]{:S(2)}, u32[]{:S(2)}) collective-permute-start(bf16[6,256,256]{2,1,0:T(8,128)(2,1)S(1)} %get-tuple-element.20), channel_id=1, source_target_pairs={{16,0},{32,16},{48,32},{64,48},{80,64},{96,80},{112,96},{0,112},{1... | collective-permute-start | bytes 2359304 | tf_op jit(solution)/shard_map/ppermute | solution.py:22
  170.7 5.9 %slice-start = ((s8[5898240]{0:T(1024)(128)(4,1)}), s8[4194304]{0:T(1024)(128)(4,1)S(1)}, s32[]{:S(2)}) async-start(s8[5898240]{0:T(1024)(128)(4,1)} %bitcast.116), calls=%async_computation.2 | async-start | bytes 8388608
  172.9 3.7 slice-start.1
  177.0 1.3 copy-start.1
  234.3 39.4 %slice-start.2 = ((s8[5898240]{0:T(1024)(128)(4,1)}), s8[4194304]{0:T(1024)(128)(4,1)S(1)}, s32[]{:S(2)}) async-start(s8[5898240]{0:T(1024)(128)(4,1)} %bitcast.118), calls=%async_computation.4 | async-start | bytes 8388608
  235.9 32.8 %collective-permute-start.2 = (bf16[6,256,256]{2,1,0:T(8,128)(2,1)S(1)}, bf16[6,256,256]{2,1,0:T(8,128)(2,1)S(1)}, u32[]{:S(2)}, u32[]{:S(2)}) collective-permute-start(bf16[6,256,256]{2,1,0:T(8,128)(2,1)S(1)} %get-tuple-element.17), channel_id=1, source_target_pairs={{0,16},{16,32},{32,48},{48,64},{64,80},{80,96},{96,112},{112,0},{1... | collective-permute-start | bytes 2359304 | tf_op jit(solution)/shard_map/ppermute | solution.py:21
  236.0 37.7 %slice-start.3 = ((s8[5898240]{0:T(1024)(128)(4,1)}), s8[1703936]{0:T(1024)(128)(4,1)S(1)}, s32[]{:S(2)}) async-start(s8[5898240]{0:T(1024)(128)(4,1)} %bitcast.118), calls=%async_computation.5 | async-start | bytes 3407872
  236.0 34.3 %collective-permute-start.3 = (bf16[6,256,256]{2,1,0:T(8,128)(2,1)S(1)}, bf16[6,256,256]{2,1,0:T(8,128)(2,1)S(1)}, u32[]{:S(2)}, u32[]{:S(2)}) collective-permute-start(bf16[6,256,256]{2,1,0:T(8,128)(2,1)S(1)} %get-tuple-element.18), channel_id=1, source_target_pairs={{16,0},{32,16},{48,32},{64,48},{80,64},{96,80},{112,96},{0,112},{1... | collective-permute-start | bytes 2359304 | tf_op jit(solution)/shard_map/ppermute | solution.py:22
  274.6 1.3 copy-start.2
  274.6 2.0 copy-start.3
